TPU v7x, 256 devices: a whole 4x4x8 slice. The times are simulated.
256 devices in a mesh: dp: 16 (over y, z_hi), expert: 8 (over x, core), tensor: 2 (over z_lo).
Axes of the slice: x: 4, y: 4, z: 8 (z_hi: 4, z_lo: 2; z = z_hi * 2 + z_lo), core: 2. Of those that a mesh axis runs over, the one named last changes fastest.
Arguments:
- tokens: bfloat16 [2048, 5120], P('dp', 'tensor'), may hold values from -6 to 6
- routes: int32 [2048, 6], P('dp'), may hold values from 0 to 15, all different within a row; in each aligned block of 128 rows (0 to 127, 128 to 255, ...) at most 72 rows name the same one
- route_weights: float32 [2048, 6], P('dp'), may hold values from 0.05 to 0.5
- gate_weight: bfloat16 [16, 1536, 5120], P('dp', 'expert', 'tensor'), may hold values from -0.078125 to 0.078125
- up_weight: bfloat16 [16, 1536, 5120], P('dp', 'expert', 'tensor'), may hold values from -0.078125 to 0.078125
- down_weight: bfloat16 [16, 1536, 5120], P('dp', 'expert', 'tensor'), may hold values from -0.15625 to 0.15625
- cotangent: bfloat16 [2048, 5120], P('dp', 'tensor'), may hold values from -6 to 6
Outputs:
- layer_out: bfloat16 [2048, 5120], P('dp', 'tensor')
- token_grad: bfloat16 [2048, 5120], P('dp', 'tensor')
- gate_grad: float32 [16, 1536, 5120], P('dp', 'expert', 'tensor')
- up_grad: float32 [16, 1536, 5120], P('dp', 'expert', 'tensor')
- down_grad: float32 [16, 1536, 5120], P('dp', 'expert', 'tensor')
Inputs may be any that keep to these rules, and one draw needn't show every extreme that they name: `routes`: each row names 6 different experts. In the rows of one index of dp (aligned blocks of 128 rows) no expert is named by more than 72 rows, a bound that some block reaches.
All inputs are finite; a program needn't handle non-finite values.
Results may differ from a plain program's by a relative error of at most 0.023.
Values may be sent and summed in bfloat16 or wider, within the bound.
A program may use at most 128 MiB of HBM per device.

v0:
```python
import jax
import jax.numpy as jnp
from jax import lax
from jax.sharding import PartitionSpec as P


def body(tokens, routes, route_weights, gate_weight, up_weight, down_weight, cotangent):
    dp_count = lax.axis_size("dp")
    hidden_split = lax.axis_size("expert")
    local_exp, hidden_share, half_width = gate_weight.shape
    tok_rows, top_count = routes.shape
    experts = local_exp * dp_count
    capacity = min(tok_rows, 3 * tok_rows * top_count // (2 * experts))
    share_rows = capacity // hidden_split
    pair_count = tok_rows * top_count
    slot_count = experts * capacity
    flat_route = routes.reshape(pair_count)
    onehot = (flat_route[:, None] == jnp.arange(experts, dtype=jnp.int32)[None, :]).astype(
        jnp.int32
    )
    position = jnp.sum((jnp.cumsum(onehot, axis=0) - 1) * onehot, axis=1)
    target = flat_route * capacity + position
    selector = jnp.arange(slot_count, dtype=jnp.int32)[:, None] == target[None, :]
    place_tok = jnp.any(selector.reshape(slot_count, tok_rows, top_count), axis=2).astype(
        jnp.bfloat16
    )
    flat_weight = route_weights.reshape(pair_count)
    slot_weight = jnp.sum(jnp.where(selector, flat_weight[None, :], jnp.float32(0.0)), axis=1)
    pair_token = jnp.arange(pair_count, dtype=jnp.int32) // top_count
    slot_token = jnp.sum(jnp.where(selector, pair_token[None, :], 0), axis=1)
    slot_used = jnp.any(selector, axis=1)
    slot_token = jnp.where(slot_used, slot_token, tok_rows)
    own_start = lax.axis_index("expert") * share_rows
    own_place = lax.dynamic_slice_in_dim(
        place_tok.reshape(experts, capacity, tok_rows), own_start, share_rows, 1
    )
    own_place = own_place.reshape(experts * share_rows, tok_rows)
    own_weight = lax.dynamic_slice_in_dim(
        slot_weight.reshape(experts, capacity), own_start, share_rows, 1
    )
    own_weight = own_weight.reshape(experts * share_rows)
    own_token = lax.dynamic_slice_in_dim(
        slot_token.reshape(experts, capacity), own_start, share_rows, 1
    )
    own_token = own_token.reshape(experts * share_rows)

    def send_rows(slot_rows):
        slot_grid = slot_rows.reshape(dp_count, local_exp, capacity, half_width)
        arrived = lax.all_to_all(slot_grid, "dp", split_axis=0, concat_axis=2, tiled=True)
        return arrived.reshape(local_exp, dp_count, capacity, half_width)

    def width_sum(partial_values):
        return lax.psum(partial_values.astype(jnp.bfloat16), "tensor").astype(jnp.float32)

    def reduce_rows(partial_rows):
        slot_grid = partial_rows.reshape(local_exp, dp_count, capacity, half_width)
        summed = lax.psum_scatter(
            slot_grid.astype(jnp.bfloat16), "expert", scatter_dimension=2, tiled=True
        )
        return summed

    def send_home(share_block):
        returned = lax.all_to_all(share_block, "dp", split_axis=1, concat_axis=0, tiled=True)
        return returned.reshape(experts * share_rows, half_width)

    def token_sum(partial_tokens):
        return lax.psum(partial_tokens.astype(jnp.bfloat16), "expert").astype(jnp.float32)

    token_slots = jnp.dot(place_tok, tokens, preferred_element_type=jnp.float32).astype(
        jnp.bfloat16
    )
    rows = send_rows(token_slots)
    flat_rows = rows.reshape(local_exp, dp_count * capacity, half_width)
    gate_part = jnp.einsum(
        "lrd,lfd->lrf", flat_rows, gate_weight, preferred_element_type=jnp.float32
    )
    up_part = jnp.einsum("lrd,lfd->lrf", flat_rows, up_weight, preferred_element_type=jnp.float32)
    both_values = width_sum(jnp.stack((gate_part, up_part)))
    gate_val = both_values[0]
    up_val = both_values[1]
    sigmoid_gate = jax.nn.sigmoid(gate_val)
    activated = gate_val * sigmoid_gate
    hidden = (activated * up_val).astype(jnp.bfloat16)
    down_part = jnp.einsum("lrf,lfd->lrd", hidden, down_weight, preferred_element_type=jnp.float32)
    expert_out = send_home(reduce_rows(down_part))
    weighted = own_weight[:, None] * expert_out.astype(jnp.float32)
    out_part = (
        jnp.zeros((tok_rows, half_width), jnp.float32).at[own_token].add(weighted, mode="drop")
    )
    layer_out = token_sum(out_part).astype(jnp.bfloat16)
    pair_grad = (
        flat_weight[:, None] * jnp.repeat(cotangent, top_count, axis=0).astype(jnp.float32)
    ).astype(jnp.bfloat16)
    grad_slots = jnp.dot(
        selector.astype(jnp.bfloat16), pair_grad, preferred_element_type=jnp.float32
    ).astype(jnp.bfloat16)
    grad_rows = send_rows(grad_slots).reshape(local_exp, dp_count * capacity, half_width)
    hidden_grad = width_sum(
        jnp.einsum("lrd,lfd->lrf", grad_rows, down_weight, preferred_element_type=jnp.float32)
    )
    gate_delta = (
        hidden_grad * up_val * sigmoid_gate * (1.0 + gate_val * (1.0 - sigmoid_gate))
    ).astype(jnp.bfloat16)
    up_delta = (hidden_grad * activated).astype(jnp.bfloat16)
    input_part = jnp.einsum(
        "lrf,lfd->lrd", gate_delta, gate_weight, preferred_element_type=jnp.float32
    )
    input_part = input_part + jnp.einsum(
        "lrf,lfd->lrd", up_delta, up_weight, preferred_element_type=jnp.float32
    )
    row_grad = send_home(reduce_rows(input_part))
    grad_part = jnp.einsum("st,sd->td", own_place, row_grad, preferred_element_type=jnp.float32)
    token_grad = token_sum(grad_part).astype(jnp.bfloat16)
    gate_grad = jnp.einsum(
        "lrf,lrd->lfd", gate_delta, flat_rows, preferred_element_type=jnp.float32
    )
    up_grad = jnp.einsum("lrf,lrd->lfd", up_delta, flat_rows, preferred_element_type=jnp.float32)
    down_grad = jnp.einsum("lrf,lrd->lfd", hidden, grad_rows, preferred_element_type=jnp.float32)
    return (layer_out, token_grad, gate_grad, up_grad, down_grad)


def solution(mesh):
    in_specs = (
        P("dp", "tensor"),
        P("dp", None),
        P("dp", None),
        P("dp", "expert", "tensor"),
        P("dp", "expert", "tensor"),
        P("dp", "expert", "tensor"),
        P("dp", "tensor"),
    )
    out_specs = (
        P("dp", "tensor"),
        P("dp", "tensor"),
        P("dp", "expert", "tensor"),
        P("dp", "expert", "tensor"),
        P("dp", "expert", "tensor"),
    )
    return jax.shard_map(body, mesh=mesh, in_specs=in_specs, out_specs=out_specs, check_vma=False)
```

profile of v0, /device:TPU:8, one launch (start us, length us, event | category | flops | bytes accessed | tf_op | source)
XLA Modules:
  0.0 626.3 jit_solution(9417354293102109201)
XLA Ops:
  12.0 5.4 convolution_convert_fusion.1
  17.3 11.7 %all-to-all-start = ((bf16[16,1,72,2560]{3,2,1,0:T(8,128)(2,1)}), bf16[16,1,72,2560]{3,2,1,0:T(8,128)(2,1)}, u32[]{:S(2)}, u32[]{:S(2)}) async-start(bf16[16,1,72,2560]{3,2,1,0:T(8,128)(2,1)} %bitcast.114), calls=%async_computation | async-start | bytes 11796480 | tf_op jit(solution)/shard_map/all_to_all | solution.py:49
  29.3 5.3 broadcast_in_dim.48
  34.6 9.5 %convert_element_type.111 = f32[768,2560]{1,0:T(8,128)} reshape(f32[128,6,2560]{2,1,0:T(8,128)} %broadcast_in_dim.48) | data formatting | bytes 15728640 | tf_op jit(solution)/shard_map/convert_element_type | solution.py:92
  44.1 9.9 %convolution_convert_fusion = bf16[1152,2560]{1,0:T(8,128)(2,1)} fusion(f32[768,2560]{1,0:T(8,128)} %convert_element_type.111, f32[768]{0:T(1024)S(1)} %broadcast_in_dim.45, s32[768]{0:T(1024)S(1)} %get-tuple-element.10), kind=kOutput, calls=%fused_computation.2 | convolution fusion | flops 4537614336 | bytes 13768704 | tf_op jit(solution)/shard_map/dot_general | solution.py:94
  54.0 108.3 %all-to-all-done = bf16[16,1,72,2560]{3,2,1,0:T(8,128)(2,1)} async-done(((bf16[16,1,72,2560]{3,2,1,0:T(8,128)(2,1)}), bf16[16,1,72,2560]{3,2,1,0:T(8,128)(2,1)}, u32[]{:S(2)}, u32[]{:S(2)}) %all-to-all-start) | async-done | bytes 5898272 | tf_op jit(solution)/shard_map/all_to_all | solution.py:49
  162.3 6.2 all-to-all-start.2
  168.6 5.1 fusion.6
  173.7 4.7 fusion.5
  179.4 103.4 %all-to-all-done.2 = bf16[16,1,72,2560]{3,2,1,0:T(8,128)(2,1)} async-done(((bf16[16,1,72,2560]{3,2,1,0:T(8,128)(2,1)}), bf16[16,1,72,2560]{3,2,1,0:T(8,128)(2,1)}, u32[]{:S(2)}, u32[]{:S(2)}) %all-to-all-start.2) | async-done | bytes 5898272 | tf_op jit(solution)/shard_map/all_to_all | solution.py:49
  282.9 5.5 fusion.7
  288.6 112.7 %all-reduce.7.cloned.1.call-done = (bf16[2,1,1152,192]{2,3,1,0:T(8,128)(2,1)}, bf16[1,1152,192]{1,2,0:T(8,128)(2,1)}) async-done(((bf16[2,1,1152,192]{2,3,1,0:T(8,128)(2,1)}, bf16[1,1152,192]{1,2,0:T(8,128)(2,1)}), (bf16[2,1,1152,192]{2,3,1,0:T(8,128)(2,1)}, bf16[1,1152,192]{1,2,0:T(8,128)(2,1)})) %all-reduce.7.cloned.1.call-update) | async-done | bytes 1327120 | tf_op jit(solution)/shard_map/psum | solution.py:53
  406.7 4.3 copy.55
  417.3 4.4 copy.58
  421.7 33.9 %reduce-scatter.3.cloned.1.call-done = bf16[1,16,9,2560]{3,1,0,2:T(8,128)(2,1)} async-done(((bf16[1,16,72,2560]{3,1,0,2:T(8,128)(2,1)}), bf16[1,16,9,2560]{3,1,0,2:T(8,128)(2,1)}) %reduce-scatter.3.cloned.1.call-update) | async-done | bytes 737296 | tf_op jit(solution)/shard_map/reduce_scatter | solution.py:57
  458.2 10.0 %all-to-all-start.1 = ((bf16[1,16,9,2560]{3,2,0,1:T(8,128)(2,1)}), bf16[1,16,9,2560]{3,2,0,1:T(8,128)(2,1)}, u32[]{:S(2)}, u32[]{:S(2)}) async-start(bf16[1,16,9,2560]{3,2,0,1:T(8,128)(2,1)} %copy.56), calls=%async_computation.2 | async-start | bytes 2621440 | tf_op jit(solution)/shard_map/all_to_all | solution.py:63
  469.1 33.4 %reduce-scatter.5.cloned.1.call-done = bf16[1,16,9,2560]{3,1,0,2:T(8,128)(2,1)} async-done(((bf16[1,16,72,2560]{3,1,0,2:T(8,128)(2,1)}), bf16[1,16,9,2560]{3,1,0,2:T(8,128)(2,1)}) %reduce-scatter.5.cloned.1.call-update) | async-done | bytes 737296 | tf_op jit(solution)/shard_map/reduce_scatter | solution.py:57
  505.1 10.0 %all-to-all-start.3 = ((bf16[1,16,9,2560]{3,2,0,1:T(8,128)(2,1)}), bf16[1,16,9,2560]{3,2,0,1:T(8,128)(2,1)}, u32[]{:S(2)}, u32[]{:S(2)}) async-start(bf16[1,16,9,2560]{3,2,0,1:T(8,128)(2,1)} %copy.59), calls=%async_computation.5 | async-start | bytes 2621440 | tf_op jit(solution)/shard_map/all_to_all | solution.py:63
  517.0 5.4 convolution_bitcast_fusion
  525.1 4.7 scatter_custom_fusion
  532.1 14.4 %all-to-all-done.3 = bf16[1,16,9,2560]{3,2,0,1:T(8,128)(2,1)} async-done(((bf16[1,16,9,2560]{3,2,0,1:T(8,128)(2,1)}), bf16[1,16,9,2560]{3,2,0,1:T(8,128)(2,1)}, u32[]{:S(2)}, u32[]{:S(2)}) %all-to-all-start.3) | async-done | bytes 737312 | tf_op jit(solution)/shard_map/all_to_all | solution.py:63
  549.4 5.4 convolution_bitcast_fusion.2
  554.8 5.5 convolution_bitcast_fusion.1
  560.3 55.5 %all-reduce.5.cloned.1.call-done = (bf16[128,2560]{1,0:T(8,128)(2,1)}, bf16[128,2560]{1,0:T(8,128)(2,1)}) async-done(((bf16[128,2560]{1,0:T(8,128)(2,1)}, bf16[128,2560]{1,0:T(8,128)(2,1)}), (bf16[128,2560]{1,0:T(8,128)(2,1)}, bf16[128,2560]{1,0:T(8,128)(2,1)})) %all-reduce.5.cloned.1.call-update) | async-done | bytes 1310736 | tf_op jit(solution)/shard_map/psum | solution.py:67
  (71 shorter events, 37.6 us)
Async XLA Ops:
  7.2 275.7 %copy-start = (bf16[1,192,2560]{2,1,0:T(8,128)(2,1)S(1)}, bf16[1,192,2560]{2,1,0:T(8,128)(2,1)}, u32[]{:S(2)}) copy-start(bf16[1,192,2560]{2,1,0:T(8,128)(2,1)} %param.12) | copy-start | bytes 2949124
  12.0 5.4 copy-start.4
  17.3 11.7 %copy-start.8 = (f32[128,6]{0,1:T(8,128)S(1)}, f32[128,6]{0,1:T(8,128)}, u32[]{:S(2)}) copy-start(f32[128,6]{0,1:T(8,128)} %param.9) | copy-start | bytes 9220
  17.3 12.0 %copy-start.7 = (bf16[128,2560]{1,0:T(8,128)(2,1)S(1)}, bf16[128,2560]{1,0:T(8,128)(2,1)}, u32[]{:S(2)}) copy-start(bf16[128,2560]{1,0:T(8,128)(2,1)} %param.13) | copy-start | bytes 1966084
  17.3 144.9 %all-to-all-start = ((bf16[16,1,72,2560]{3,2,1,0:T(8,128)(2,1)}), bf16[16,1,72,2560]{3,2,1,0:T(8,128)(2,1)}, u32[]{:S(2)}, u32[]{:S(2)}) async-start(bf16[16,1,72,2560]{3,2,1,0:T(8,128)(2,1)} %bitcast.114), calls=%async_computation | async-start | bytes 11796480 | tf_op jit(solution)/shard_map/all_to_all | solution.py:49
  162.3 120.6 %all-to-all-start.2 = ((bf16[16,1,72,2560]{3,2,1,0:T(8,128)(2,1)}), bf16[16,1,72,2560]{3,2,1,0:T(8,128)(2,1)}, u32[]{:S(2)}, u32[]{:S(2)}) async-start(bf16[16,1,72,2560]{3,2,1,0:T(8,128)(2,1)} %bitcast.116), calls=%async_computation.3 | async-start | bytes 11796480 | tf_op jit(solution)/shard_map/all_to_all | solution.py:49
  168.5 232.8 %all-reduce.7.cloned.1.call-start = ((), (), s32[]{:S(2)}) async-start(), calls=%async_computation.9 | async-start | bytes 2654208 | tf_op jit(solution)/shard_map/psum | solution.py:53
  168.6 5.1 copy-start.5
  288.4 167.2 %reduce-scatter.3.cloned.1.call-start = ((), (), s32[]{:S(2)}) async-start(), calls=%async_computation.6 | async-start | bytes 6635520 | tf_op jit(solution)/shard_map/reduce_scatter | solution.py:57
  411.0 1.0 copy-start.2
  411.0 91.5 %reduce-scatter.5.cloned.1.call-start = ((), (), s32[]{:S(2)}) async-start(), calls=%async_computation.7 | async-start | bytes 6635520 | tf_op jit(solution)/shard_map/reduce_scatter | solution.py:57
  412.4 3.0 copy-start.6
  458.2 46.9 %all-to-all-start.1 = ((bf16[1,16,9,2560]{3,2,0,1:T(8,128)(2,1)}), bf16[1,16,9,2560]{3,2,0,1:T(8,128)(2,1)}, u32[]{:S(2)}, u32[]{:S(2)}) async-start(bf16[1,16,9,2560]{3,2,0,1:T(8,128)(2,1)} %copy.56), calls=%async_computation.2 | async-start | bytes 2621440 | tf_op jit(solution)/shard_map/all_to_all | solution.py:63
  505.1 41.4 %all-to-all-start.3 = ((bf16[1,16,9,2560]{3,2,0,1:T(8,128)(2,1)}), bf16[1,16,9,2560]{3,2,0,1:T(8,128)(2,1)}, u32[]{:S(2)}, u32[]{:S(2)}) async-start(bf16[1,16,9,2560]{3,2,0,1:T(8,128)(2,1)} %copy.59), calls=%async_computation.5 | async-start | bytes 2621440 | tf_op jit(solution)/shard_map/all_to_all | solution.py:63
  515.1 100.7 %all-reduce.5.cloned.1.call-start = ((), (), s32[]{:S(2)}) async-start(), calls=%async_computation.8 | async-start | bytes 2621440 | tf_op jit(solution)/shard_map/psum | solution.py:67
  549.4 5.4 copy-start.3
  554.8 65.0 %copy-start.1 = (bf16[1,192,2560]{2,1,0:T(8,128)(2,1)S(1)}, bf16[1,192,2560]{2,1,0:T(8,128)(2,1)}, u32[]{:S(2)}) copy-start(bf16[1,192,2560]{2,1,0:T(8,128)(2,1)} %param.12) | copy-start | bytes 2949124
Sparse Core Ops, SparseCore 0:
  288.5 112.7 all-reduce.6
  411.2 44.3 reduce-scatter.2
  458.1 44.3 reduce-scatter.4
  549.5 66.3 all-reduce.4
where the time goes:
time: 628 us; the launch traced here: 626 us
  waiting for transfers between devices  462 us (74%)
  matrix products  55.8 us (9%)
  local copies, waits for them, and re-layouts  42.2 us (7%)
  starting transfers between devices  38.3 us (6%)
  other arithmetic  14.3 us (2%)
  between operations  14 us (2%)
    all_to_all x2, waiting for transfers between devices, send_rows(): lax.all_to_all(slot_grid, 'dp', split_axis=0, concat_axis=2, tiled=True)  212 us
    psum x1, waiting for transfers between devices, width_sum(): lax.psum(partial_values.astype(jnp.bfloat16), 'tensor').astype(jnp.float32)  113 us
    reduce_scatter x2, waiting for transfers between devices, reduce_rows(): lax.psum_scatter(slot_grid.astype(jnp.bfloat16), 'expert', scatter_dimens...  67.3 us
    psum x1, waiting for transfers between devices, token_sum(): lax.psum(partial_tokens.astype(jnp.bfloat16), 'expert').astype(jnp.float32)  55.5 us
    all_to_all x2, starting transfers between devices, send_home(): lax.all_to_all(share_block, 'dp', split_axis=1, concat_axis=0, tiled=True)  20 us
    all_to_all x2, starting transfers between devices, send_rows(): lax.all_to_all(slot_grid, 'dp', split_axis=0, concat_axis=2, tiled=True)  17.9 us
    all_to_all x2, waiting for transfers between devices, send_home(): lax.all_to_all(share_block, 'dp', split_axis=1, concat_axis=0, tiled=True)  14.4 us
  transfers between devices with their start and end apart: 8, of which 7 were waited for; matrix products, arithmetic and copies ran while one was open for 13% of the time, Pallas kernels for 0%

commit v1 on v0

--- a/solution.py
+++ b/solution.py
@@ -50,7 +50,9 @@
         return arrived.reshape(local_exp, dp_count, capacity, half_width)
 
     def width_sum(partial_values):
-        return lax.psum(partial_values.astype(jnp.bfloat16), "tensor").astype(jnp.float32)
+        return jnp.sum(
+            lax.all_gather(partial_values.astype(jnp.bfloat16), "tensor"), axis=0
+        ).astype(jnp.float32)
 
     def reduce_rows(partial_rows):
         slot_grid = partial_rows.reshape(local_exp, dp_count, capacity, half_width)

time: 628 us -> 582 us (0.927)
  waiting for transfers between devices: 462 us -> 376 us
  blocking collectives: 0 us -> 33.6 us
  other arithmetic: 14.3 us -> 22 us
    psum x1 -> x0, waiting for transfers between devices: 113 us -> none  [width_sum(): lax.psum(partial_values.astype(jnp.bfloat16), 'tensor').astype(jnp.float32)]
    all_gather x0 -> x1, blocking collectives: none -> 33.6 us  [width_sum(): lax.all_gather(partial_values.astype(jnp.bfloat16), 'tensor')]
    all_to_all x2, waiting for transfers between devices: 212 us -> 242 us  [send_rows(): lax.all_to_all(slot_grid, 'dp', split_axis=0, concat_axis=2, tiled=True)]
  transfers between devices with their start and end apart: 8 -> 8, of which waited for: 7 -> 6; matrix products, arithmetic and copies ran while one was open for 13% -> 15% of each run, Pallas kernels for 0% -> 0%
where the time goes in v1:
time: 582 us; the launch traced here: 581 us
  waiting for transfers between devices  376 us (65%)
  matrix products  54.7 us (9%)
  local copies, waits for them, and re-layouts  42.5 us (7%)
  starting transfers between devices  38.5 us (7%)
  blocking collectives  33.6 us (6%)
  other arithmetic  22 us (4%)
  between operations  14 us (2%)
    all_to_all x2, waiting for transfers between devices, send_rows(): lax.all_to_all(slot_grid, 'dp', split_axis=0, concat_axis=2, tiled=True)  242 us
    reduce_scatter x2, waiting for transfers between devices, reduce_rows(): lax.psum_scatter(slot_grid.astype(jnp.bfloat16), 'expert', scatter_dimens...  63.1 us
    psum x1, waiting for transfers between devices, token_sum(): lax.psum(partial_tokens.astype(jnp.bfloat16), 'expert').astype(jnp.float32)  55.5 us
    all_gather x1, blocking collectives, width_sum(): lax.all_gather(partial_values.astype(jnp.bfloat16), 'tensor')  33.6 us
    all_to_all x2, starting transfers between devices, send_home(): lax.all_to_all(share_block, 'dp', split_axis=1, concat_axis=0, tiled=True)  20 us
    all_to_all x2, starting transfers between devices, send_rows(): lax.all_to_all(slot_grid, 'dp', split_axis=0, concat_axis=2, tiled=True)  18.1 us
    all_to_all x2, waiting for transfers between devices, send_home(): lax.all_to_all(share_block, 'dp', split_axis=1, concat_axis=0, tiled=True)  14.6 us
  transfers between devices with their start and end apart: 8, of which 6 were waited for; matrix products, arithmetic and copies ran while one was open for 15% of the time, Pallas kernels for 0%

profile of v1, /device:TPU:8, one launch (start us, length us, event | category | flops | bytes accessed | tf_op | source)
XLA Modules:
  0.0 580.9 jit_solution(12378762998732764299)
XLA Ops:
  12.0 5.4 convolution_convert_fusion.1
  17.3 11.7 %all-to-all-start = ((bf16[16,1,72,2560]{3,2,1,0:T(8,128)(2,1)}), bf16[16,1,72,2560]{3,2,1,0:T(8,128)(2,1)}, u32[]{:S(2)}, u32[]{:S(2)}) async-start(bf16[16,1,72,2560]{3,2,1,0:T(8,128)(2,1)} %bitcast.109), calls=%async_computation | async-start | bytes 11796480 | tf_op jit(solution)/shard_map/all_to_all | solution.py:49
  29.3 5.3 broadcast_in_dim.48
  34.6 9.5 %convert_element_type.169 = f32[768,2560]{1,0:T(8,128)} reshape(f32[128,6,2560]{2,1,0:T(8,128)} %broadcast_in_dim.48) | data formatting | bytes 15728640 | tf_op jit(solution)/shard_map/convert_element_type | solution.py:94
  44.1 9.9 %convolution_convert_fusion = bf16[1152,2560]{1,0:T(8,128)(2,1)} fusion(f32[768,2560]{1,0:T(8,128)} %convert_element_type.169, f32[768]{0:T(1024)S(1)} %broadcast_in_dim.45, s32[768]{0:T(1024)S(1)} %get-tuple-element.10), kind=kOutput, calls=%fused_computation.2 | convolution fusion | flops 4537614336 | bytes 13768704 | tf_op jit(solution)/shard_map/dot_general | solution.py:96
  54.0 108.3 %all-to-all-done = bf16[16,1,72,2560]{3,2,1,0:T(8,128)(2,1)} async-done(((bf16[16,1,72,2560]{3,2,1,0:T(8,128)(2,1)}), bf16[16,1,72,2560]{3,2,1,0:T(8,128)(2,1)}, u32[]{:S(2)}, u32[]{:S(2)}) %all-to-all-start) | async-done | bytes 5898272 | tf_op jit(solution)/shard_map/all_to_all | solution.py:49
  162.3 6.4 %all-to-all-start.2 = ((bf16[16,1,72,2560]{3,2,1,0:T(8,128)(2,1)}), bf16[16,1,72,2560]{3,2,1,0:T(8,128)(2,1)}, u32[]{:S(2)}, u32[]{:S(2)}) async-start(bf16[16,1,72,2560]{3,2,1,0:T(8,128)(2,1)} %bitcast.111), calls=%async_computation.3 | async-start | bytes 11796480 | tf_op jit(solution)/shard_map/all_to_all | solution.py:49
  168.7 4.8 fusion.6
  173.6 4.7 fusion.5
  179.4 134.0 %all-to-all-done.2 = bf16[16,1,72,2560]{3,2,1,0:T(8,128)(2,1)} async-done(((bf16[16,1,72,2560]{3,2,1,0:T(8,128)(2,1)}), bf16[16,1,72,2560]{3,2,1,0:T(8,128)(2,1)}, u32[]{:S(2)}, u32[]{:S(2)}) %all-to-all-start.2) | async-done | bytes 5898272 | tf_op jit(solution)/shard_map/all_to_all | solution.py:49
  313.3 4.7 convolution_convert_fusion.4
  318.1 33.6 %all-gather = bf16[2304,192]{0,1:T(8,128)(2,1)S(1)} all-gather(bf16[1152,192]{0,1:T(8,128)(2,1)S(1)} %convolution_convert_fusion.4), channel_id=2, replica_groups=mesh['dp'=16,'expert'=8,'tensor'=2] {'tensor'}, dimensions={0}, use_global_device_ids=true | all-gather | bytes 1327104 | tf_op jit(solution)/shard_map/all_gather | solution.py:54
  366.3 4.3 copy.66
  375.8 4.4 copy.69
  380.2 29.7 %reduce-scatter.3.cloned.1.call-done = bf16[1,16,9,2560]{3,1,0,2:T(8,128)(2,1)} async-done(((bf16[1,16,72,2560]{3,1,0,2:T(8,128)(2,1)}), bf16[1,16,9,2560]{3,1,0,2:T(8,128)(2,1)}) %reduce-scatter.3.cloned.1.call-update) | async-done | bytes 737296 | tf_op jit(solution)/shard_map/reduce_scatter | solution.py:59
  412.5 10.2 %all-to-all-start.1 = ((bf16[1,16,9,2560]{3,2,0,1:T(8,128)(2,1)}), bf16[1,16,9,2560]{3,2,0,1:T(8,128)(2,1)}, u32[]{:S(2)}, u32[]{:S(2)}) async-start(bf16[1,16,9,2560]{3,2,0,1:T(8,128)(2,1)} %copy.67), calls=%async_computation.2 | async-start | bytes 2621440 | tf_op jit(solution)/shard_map/all_to_all | solution.py:65
  423.6 33.4 %reduce-scatter.5.cloned.1.call-done = bf16[1,16,9,2560]{3,1,0,2:T(8,128)(2,1)} async-done(((bf16[1,16,72,2560]{3,1,0,2:T(8,128)(2,1)}), bf16[1,16,9,2560]{3,1,0,2:T(8,128)(2,1)}) %reduce-scatter.5.cloned.1.call-update) | async-done | bytes 737296 | tf_op jit(solution)/shard_map/reduce_scatter | solution.py:59
  459.7 9.9 %all-to-all-start.3 = ((bf16[1,16,9,2560]{3,2,0,1:T(8,128)(2,1)}), bf16[1,16,9,2560]{3,2,0,1:T(8,128)(2,1)}, u32[]{:S(2)}, u32[]{:S(2)}) async-start(bf16[1,16,9,2560]{3,2,0,1:T(8,128)(2,1)} %copy.70), calls=%async_computation.5 | async-start | bytes 2621440 | tf_op jit(solution)/shard_map/all_to_all | solution.py:65
  471.5 5.4 convolution_bitcast_fusion
  479.6 4.7 scatter_custom_fusion
  486.5 14.6 %all-to-all-done.3 = bf16[1,16,9,2560]{3,2,0,1:T(8,128)(2,1)} async-done(((bf16[1,16,9,2560]{3,2,0,1:T(8,128)(2,1)}), bf16[1,16,9,2560]{3,2,0,1:T(8,128)(2,1)}, u32[]{:S(2)}, u32[]{:S(2)}) %all-to-all-start.3) | async-done | bytes 737312 | tf_op jit(solution)/shard_map/all_to_all | solution.py:65
  504.0 5.4 convolution_bitcast_fusion.2
  509.4 5.5 convolution_bitcast_fusion.1
  514.9 55.5 %all-reduce.3.cloned.1.call-done = (bf16[128,2560]{1,0:T(8,128)(2,1)}, bf16[128,2560]{1,0:T(8,128)(2,1)}) async-done(((bf16[128,2560]{1,0:T(8,128)(2,1)}, bf16[128,2560]{1,0:T(8,128)(2,1)}), (bf16[128,2560]{1,0:T(8,128)(2,1)}, bf16[128,2560]{1,0:T(8,128)(2,1)})) %all-reduce.3.cloned.1.call-update) | async-done | bytes 1310736 | tf_op jit(solution)/shard_map/psum | solution.py:69
  (78 shorter events, 45.7 us)
Async XLA Ops:
  7.2 306.2 %copy-start = (bf16[1,192,2560]{2,1,0:T(8,128)(2,1)S(1)}, bf16[1,192,2560]{2,1,0:T(8,128)(2,1)}, u32[]{:S(2)}) copy-start(bf16[1,192,2560]{2,1,0:T(8,128)(2,1)} %param.12) | copy-start | bytes 2949124
  12.0 5.4 copy-start.5
  17.3 11.7 %copy-start.10 = (f32[128,6]{0,1:T(8,128)S(1)}, f32[128,6]{0,1:T(8,128)}, u32[]{:S(2)}) copy-start(f32[128,6]{0,1:T(8,128)} %param.9) | copy-start | bytes 9220
  17.3 12.0 %copy-start.9 = (bf16[128,2560]{1,0:T(8,128)(2,1)S(1)}, bf16[128,2560]{1,0:T(8,128)(2,1)}, u32[]{:S(2)}) copy-start(bf16[128,2560]{1,0:T(8,128)(2,1)} %param.13) | copy-start | bytes 1966084
  17.3 144.9 %all-to-all-start = ((bf16[16,1,72,2560]{3,2,1,0:T(8,128)(2,1)}), bf16[16,1,72,2560]{3,2,1,0:T(8,128)(2,1)}, u32[]{:S(2)}, u32[]{:S(2)}) async-start(bf16[16,1,72,2560]{3,2,1,0:T(8,128)(2,1)} %bitcast.109), calls=%async_computation | async-start | bytes 11796480 | tf_op jit(solution)/shard_map/all_to_all | solution.py:49
  162.3 6.4 %copy-start.7 = (bf16[1,192,2560]{2,1,0:T(8,128)(2,1)S(1)}, bf16[1,192,2560]{2,1,0:T(8,128)(2,1)}, u32[]{:S(2)}) copy-start(bf16[1,192,2560]{2,1,0:T(8,128)(2,1)} %param.11) | copy-start | bytes 2949124
  162.3 151.1 %all-to-all-start.2 = ((bf16[16,1,72,2560]{3,2,1,0:T(8,128)(2,1)}), bf16[16,1,72,2560]{3,2,1,0:T(8,128)(2,1)}, u32[]{:S(2)}, u32[]{:S(2)}) async-start(bf16[16,1,72,2560]{3,2,1,0:T(8,128)(2,1)} %bitcast.111), calls=%async_computation.3 | async-start | bytes 11796480 | tf_op jit(solution)/shard_map/all_to_all | solution.py:49
  168.7 186.4 %all-gather.3.cloned.1.call-start = ((), (), s32[]{:S(2)}) async-start(), calls=%async_computation.6 | async-start | bytes 2654208 | tf_op jit(solution)/shard_map/all_gather | solution.py:54
  168.7 4.8 copy-start.6
  179.3 230.6 %reduce-scatter.3.cloned.1.call-start = ((), (), s32[]{:S(2)}) async-start(), calls=%async_computation.7 | async-start | bytes 6635520 | tf_op jit(solution)/shard_map/reduce_scatter | solution.py:59
  370.6 86.4 %reduce-scatter.5.cloned.1.call-start = ((), (), s32[]{:S(2)}) async-start(), calls=%async_computation.8 | async-start | bytes 6635520 | tf_op jit(solution)/shard_map/reduce_scatter | solution.py:59
  370.9 3.1 copy-start.3
  370.9 3.1 copy-start.8
  412.5 58.9 %copy-start.2 = (bf16[1,1,1152,192]{2,3,1,0:T(8,128)(2,1)S(1)}, bf16[1,1,1152,192]{2,3,1,0:T(8,128)(2,1)}, u32[]{:S(2)}) copy-start(bf16[1,1,1152,192]{2,3,1,0:T(8,128)(2,1)} %get-tuple-element.8) | copy-start | bytes 1327108
  412.5 47.2 %all-to-all-start.1 = ((bf16[1,16,9,2560]{3,2,0,1:T(8,128)(2,1)}), bf16[1,16,9,2560]{3,2,0,1:T(8,128)(2,1)}, u32[]{:S(2)}, u32[]{:S(2)}) async-start(bf16[1,16,9,2560]{3,2,0,1:T(8,128)(2,1)} %copy.67), calls=%async_computation.2 | async-start | bytes 2621440 | tf_op jit(solution)/shard_map/all_to_all | solution.py:65
  459.7 41.4 %all-to-all-start.3 = ((bf16[1,16,9,2560]{3,2,0,1:T(8,128)(2,1)}), bf16[1,16,9,2560]{3,2,0,1:T(8,128)(2,1)}, u32[]{:S(2)}, u32[]{:S(2)}) async-start(bf16[1,16,9,2560]{3,2,0,1:T(8,128)(2,1)} %copy.70), calls=%async_computation.5 | async-start | bytes 2621440 | tf_op jit(solution)/shard_map/all_to_all | solution.py:65
  469.6 100.9 %all-reduce.3.cloned.1.call-start = ((), (), s32[]{:S(2)}) async-start(), calls=%async_computation.9 | async-start | bytes 2621440 | tf_op jit(solution)/shard_map/psum | solution.py:69
  504.0 5.4 copy-start.4
  509.4 65.0 %copy-start.1 = (bf16[1,192,2560]{2,1,0:T(8,128)(2,1)S(1)}, bf16[1,192,2560]{2,1,0:T(8,128)(2,1)}, u32[]{:S(2)}) copy-start(bf16[1,192,2560]{2,1,0:T(8,128)(2,1)} %param.12) | copy-start | bytes 2949124
Sparse Core Ops, SparseCore 0:
  179.4 123.7 all-gather.2
  370.7 39.1 reduce-scatter.2
  412.7 44.3 reduce-scatter.4
  504.1 66.3 all-reduce.2
